TPU v7x, 256 devices: a whole 4x4x8 slice. The times are simulated.
256 devices in a mesh: dp: 16 (over z, y_lo), tensor: 4 (over x), section: 4 (over y_hi, core).
Axes of the slice: x: 4, y: 4 (y_hi: 2, y_lo: 2; y = y_hi * 2 + y_lo), z: 8, core: 2. Of those that a mesh axis runs over, the one named last changes fastest.
Arguments:
- grad_parts: bfloat16 [4, 16, 4, 1024, 1024], P('section', 'dp', None, None, 'tensor'), may hold values from -1.5 to 1.5
- first_moment: float32 [4, 4, 1024, 1024], P('section', 'tensor', 'dp'), may hold values from -3 to 3
- second_moment: float32 [4, 4, 1024, 1024], P('section', 'tensor', 'dp'), may hold values from 0.1 to 4
- left_stat: float32 [4, 4, 1024, 1024], P('section', 'tensor', 'dp'), may hold values from -12288 to 184320
- right_stat: float32 [4, 4, 1024, 1024], P('section', 'tensor', 'dp'), may hold values from -12288 to 184320
- left_basis: float32 [4, 4, 1024, 1024], P('section', 'tensor', 'dp'), may hold values from -0.1875 to 0.1875
- right_basis: float32 [4, 4, 1024, 1024], P('section', 'tensor', 'dp'), may hold values from -0.1875 to 0.1875
- gain_grads: float32 [4, 16, 4, 2, 1024], P('section', 'dp', 'tensor'), may hold values from -1.2 to 1.2
- gain_first: float32 [4, 2, 1024], P('section'), may hold values from -3 to 3
- gain_second: float32 [4, 2, 1024], P('section'), may hold values from 0.1 to 4
- table_grads: float32 [4, 16, 32, 16], P('section', 'dp', None, 'tensor'), may hold values from -1.2 to 1.2
- table_first: float32 [32, 16], P(None, 'tensor'), may hold values from -3 to 3
- table_second: float32 [32, 16], P(None, 'tensor'), may hold values from 0.1 to 4
Outputs:
- update: float32 [4, 4, 1024, 1024], P('section', 'tensor', 'dp')
- first_next: float32 [4, 4, 1024, 1024], P('section', 'tensor', 'dp')
- second_next: float32 [4, 4, 1024, 1024], P('section', 'tensor', 'dp')
- left_next: float32 [4, 4, 1024, 1024], P('section', 'tensor', 'dp')
- right_next: float32 [4, 4, 1024, 1024], P('section', 'tensor', 'dp')
- left_rotation: float32 [4, 4, 1024, 1024], P('section', 'tensor', 'dp')
- right_rotation: float32 [4, 4, 1024, 1024], P('section', 'tensor', 'dp')
- gain_update: float32 [4, 2, 1024], P('section')
- gain_moment: float32 [4, 2, 1024], P('section')
- gain_squares: float32 [4, 2, 1024], P('section')
- table_update: float32 [32, 16], P(None, 'tensor')
- table_moment: float32 [32, 16], P(None, 'tensor')
- table_squares: float32 [32, 16], P(None, 'tensor')
All inputs are finite; a program needn't handle non-finite values.
Results may differ from a plain program's by a relative error of at most 0.014.
Values may be sent and summed in bfloat16 or wider, within the bound.
A program may use at most 64 MiB of HBM per device.

v0:
```python
import jax
import jax.numpy as jnp
from jax import lax
from jax.sharding import PartitionSpec as P

NS_ITERS = 3
beta_first = 0.9
beta_second = 0.95
beta_stat = 0.95
adam_eps = 1e-08
norm_eps = 1e-06
step_count = 10.0


def to_half(value):
    return value.astype(jnp.bfloat16)


def batched(pattern, left, right):
    return jnp.einsum(pattern, left, right, preferred_element_type=jnp.float32)


def adam_direction(first, second):
    first_hat = first / (1.0 - beta_first**step_count)
    second_hat = second / (1.0 - beta_second**step_count)
    return first_hat / (jnp.sqrt(second_hat) + adam_eps)


def local(
    grad_parts,
    first_moment,
    second_moment,
    left_stat,
    right_stat,
    left_basis,
    right_basis,
    gain_grads,
    gain_first,
    gain_second,
    table_grads,
    table_first,
    table_second,
):
    partial_value = grad_parts[0, 0]
    columns = lax.all_to_all(partial_value, "tensor", split_axis=0, concat_axis=2, tiled=True)
    summed = lax.psum_scatter(
        columns.astype(jnp.float32).astype(jnp.bfloat16), "dp", scatter_dimension=1, tiled=True
    ).astype(jnp.float32)
    grad_rows = to_half(summed)
    row_count = grad_rows.shape[1]
    offset = lax.axis_index("dp") * row_count
    left_local = to_half(left_basis[0])
    right_local = to_half(right_basis[0])
    left_full, right_full = (
        lax.all_gather(left_local, "dp", axis=1, tiled=True),
        lax.all_gather(right_local, "dp", axis=1, tiled=True),
    )
    grad_full = lax.all_gather(grad_rows, "dp", axis=1, tiled=True)
    rotated_half = to_half(batched("mik,mkj->mij", grad_rows, right_full))
    block = left_local
    rotated = jnp.swapaxes(
        lax.psum_scatter(
            batched("mkc,mkj->cmj", block, rotated_half), "dp", scatter_dimension=0, tiled=True
        ),
        0,
        1,
    )
    first_new = beta_first * first_moment[0] + (1.0 - beta_first) * rotated
    second_new = beta_second * second_moment[0] + (1.0 - beta_second) * rotated * rotated
    direction = to_half(adam_direction(first_new, second_new))
    block = left_local
    back_half = to_half(
        batched("mik,mkj->mij", block, lax.all_gather(direction, "dp", axis=1, tiled=True))
    )
    update = batched("mik,mjk->mij", back_half, right_full)
    grad_columns = lax.dynamic_slice_in_dim(grad_full, offset, row_count, 2)
    left_new = beta_stat * left_stat[0] + batched("mik,mjk->mij", grad_rows, grad_full)
    right_new = beta_stat * right_stat[0] + batched("mki,mkj->mij", grad_columns, grad_full)
    power_left = batched("mik,mkj->mij", to_half(left_new), left_full)
    power_right = batched("mik,mkj->mij", to_half(right_new), right_full)
    power = jnp.concatenate([power_left, power_right], axis=0)
    squares = lax.psum(jnp.sum(power * power, axis=(1, 2)), "dp")
    iterate = power / jnp.sqrt(squares + norm_eps)[:, None, None]
    for sweep in range(NS_ITERS):
        iterate_half = to_half(iterate)
        iterate_full = lax.all_gather(iterate_half, "dp", axis=1, tiled=True)
        gram = to_half(batched("mik,mjk->mij", iterate_half, iterate_full))
        iterate = 1.5 * iterate - 0.5 * batched("mik,mkj->mij", gram, iterate_full)
    local_mats = power_left.shape[0]
    left_rotation = iterate[:local_mats]
    right_rotation = iterate[local_mats:]
    gain_sum = lax.psum(gain_grads[0, 0, 0], ("dp", "tensor"))
    gain_moment = beta_first * gain_first[0] + (1.0 - beta_first) * gain_sum
    gain_squares = beta_second * gain_second[0] + (1.0 - beta_second) * gain_sum * gain_sum
    gain_update = adam_direction(gain_moment, gain_squares)
    table_sum = lax.psum(table_grads[0, 0], ("dp", "section"))
    table_moment = beta_first * table_first + (1.0 - beta_first) * table_sum
    table_squares = beta_second * table_second + (1.0 - beta_second) * table_sum * table_sum
    table_update = adam_direction(table_moment, table_squares)
    return (
        update[None],
        first_new[None],
        second_new[None],
        left_new[None],
        right_new[None],
        left_rotation[None],
        right_rotation[None],
        gain_update[None],
        gain_moment[None],
        gain_squares[None],
        table_update,
        table_moment,
        table_squares,
    )


def solution(mesh):
    return jax.shard_map(
        local,
        mesh=mesh,
        in_specs=(
            P("section", "dp", None, None, "tensor"),
            P("section", "tensor", "dp", None),
            P("section", "tensor", "dp", None),
            P("section", "tensor", "dp", None),
            P("section", "tensor", "dp", None),
            P("section", "tensor", "dp", None),
            P("section", "tensor", "dp", None),
            P("section", "dp", "tensor", None, None),
            P("section", None, None),
            P("section", None, None),
            P("section", "dp", None, "tensor"),
            P(None, "tensor"),
            P(None, "tensor"),
        ),
        out_specs=(
            P("section", "tensor", "dp", None),
            P("section", "tensor", "dp", None),
            P("section", "tensor", "dp", None),
            P("section", "tensor", "dp", None),
            P("section", "tensor", "dp", None),
            P("section", "tensor", "dp", None),
            P("section", "tensor", "dp", None),
            P("section", None, None),
            P("section", None, None),
            P("section", None, None),
            P(None, "tensor"),
            P(None, "tensor"),
            P(None, "tensor"),
        ),
        check_vma=False,
    )
```

profile of v0, /device:TPU:2, one launch (start us, length us, event | category | flops | bytes accessed | tf_op | source)
XLA Modules:
  0.0 1098.2 jit_solution(950655685034763806)
XLA Ops:
  7.2 0.0 reduce-scatter.4.cloned.1.call-start
  7.2 4.0 copy.47
  11.2 29.7 %all_to_all.18 = bf16[4,1024,256]{1,2,0:T(8,128)(2,1)S(1)} all-to-all(bf16[4,1024,256]{1,2,0:T(8,128)(2,1)} %bitcast.140), channel_id=1, replica_groups=mesh['dp'=16,'tensor'=4,'section'=4] {'tensor'}, dimensions={0} | all-to-all | bytes 4194304 | tf_op jit(solution)/shard_map/all_to_all | solution.py:45
  40.9 7.8 copy.50
  48.7 4.4 copy.60
  53.0 0.0 reduce-scatter.4.cloned.1.call-update
  53.1 0.0 all-gather.12.cloned.1.call-start
  53.1 77.8 %reduce-scatter.4.cloned.1.call-done = bf16[64,1024]{1,0:T(8,128)(2,1)} async-done(((bf16[1024,1024]{1,0:T(8,128)(2,1)}), bf16[64,1024]{1,0:T(8,128)(2,1)}) %reduce-scatter.4.cloned.1.call-update) | async-done | bytes 131088
  130.9 1.0 reshape_bitcast_fusion
  132.0 0.7 copy.49
  132.7 0.0 all-gather.20.cloned.1.call-start
  132.8 0.7 convert_element_type.84
  133.5 0.0 all-gather.22.cloned.1.call-start
  133.5 0.7 convert_element_type.87
  134.2 0.0 all-gather.14.cloned.1.call-start
  134.3 0.2 copy.51
  134.5 70.3 %all-gather.12.cloned.1.call-done = bf16[1,1024,1024]{2,1,0:T(8,128)(2,1)} async-done(((bf16[1,64,1024]{2,1,0:T(8,128)(2,1)}), bf16[1,1024,1024]{2,1,0:T(8,128)(2,1)}) %all-gather.12.cloned.1.call-update) | async-done | bytes 2097168 | tf_op jit(solution)/shard_map/all_gather | solution.py:58
  204.7 2.5 fusion.20
  207.2 70.5 %all-gather.20.cloned.1.call-done = bf16[1,1,1024,1024]{3,2,1,0:T(8,128)(2,1)} async-done(((bf16[1,1,64,1024]{3,2,1,0:T(8,128)(2,1)}), bf16[1,1,1024,1024]{3,2,1,0:T(8,128)(2,1)}) %all-gather.20.cloned.1.call-update) | async-done | bytes 2097168 | tf_op jit(solution)/shard_map/all_gather | solution.py:56
  277.7 2.1 fusion.26
  279.8 0.8 fusion.17
  280.6 69.9 %all-gather.22.cloned.1.call-done = bf16[1,1,1024,1024]{3,2,1,0:T(8,128)(2,1)} async-done(((bf16[1,1,64,1024]{3,2,1,0:T(8,128)(2,1)}), bf16[1,1,1024,1024]{3,2,1,0:T(8,128)(2,1)}) %all-gather.22.cloned.1.call-update) | async-done | bytes 2097168 | tf_op jit(solution)/shard_map/all_gather | solution.py:55
  350.5 2.1 fusion.29
  352.6 0.2 multiply_reduce_fusion
  352.8 32.8 %psum.21 = f32[2]{0:T(128)S(1)} all-reduce(f32[2]{0:T(128)S(1)} %multiply_reduce_fusion), channel_id=1, replica_groups=mesh['dp'=16,'tensor'=4,'section'=4] {'dp'}, use_global_device_ids=true, to_apply=%region_3.0 | all-reduce | flops 2 | bytes 16 | tf_op jit(solution)/shard_map/psum | solution.py:82
  385.6 0.8 fusion.68
  386.4 0.0 all-reduce.3.cloned.1.call-start
  386.5 3.2 convolution_bitcast_fusion
  389.7 11.0 %copy.48 = f32[1024,1,1024]{2,1,0:T(1,128)} copy(f32[1024,1,1024]{0,2,1:T(8,128)} %convolution_bitcast_fusion) | data formatting | bytes 8388608 | tf_op jit(solution)/shard_map/mkc,mkj->cmj/transpose | solution.py:20
  400.8 0.0 all-gather.16.cloned.1.call-start
  400.9 84.0 %all-gather.14.cloned.1.call-done = bf16[2,1024,1024]{2,1,0:T(8,128)(2,1)} async-done(((bf16[2,64,1024]{2,1,0:T(8,128)(2,1)}), bf16[2,1024,1024]{2,1,0:T(8,128)(2,1)}) %all-gather.14.cloned.1.call-update) | async-done | bytes 4194320 | tf_op jit(solution)/shard_map/all_gather | solution.py:86
  484.9 6.5 fusion.73
  491.4 0.0 all-gather.10.cloned.1.call-start
  491.5 0.6 dynamic-slice
  492.7 193.9 %all-reduce.3.cloned.1.call-done = f32[1024,1,1024]{2,1,0:T(1,128)} async-done(((f32[1024,1,1024]{2,1,0:T(1,128)}), f32[1024,1,1024]{2,1,0:T(1,128)}) %all-reduce.3.cloned.1.call-update) | async-done | bytes 4194320
  686.6 1.0 constant_dynamic-slice_fusion
  687.6 0.8 fusion.57
  688.5 0.0 all-gather.18.cloned.1.call-start
  688.5 99.6 %all-gather.16.cloned.1.call-done = bf16[2,1024,1024]{2,1,0:T(8,128)(2,1)} async-done(((bf16[2,64,1024]{2,1,0:T(8,128)(2,1)}), bf16[2,1024,1024]{2,1,0:T(8,128)(2,1)}) %all-gather.16.cloned.1.call-update) | async-done | bytes 4194320 | tf_op jit(solution)/shard_map/all_gather | solution.py:86
  788.1 6.4 fusion.76
  794.6 128.0 %psum.23 = f32[32,4]{0,1:T(4,128)} all-reduce(f32[32,4]{0,1:T(4,128)S(1)} %bitcast.144), channel_id=1, replica_groups=mesh['dp'=16,'tensor'=4,'section'=4] {'dp','section'}, use_global_device_ids=true, to_apply=%region_5.0 | all-reduce | flops 128 | bytes 1024 | tf_op jit(solution)/shard_map/psum | solution.py:96
  922.6 155.6 %psum.22 = f32[2,1024]{1,0:T(2,128)S(1)} all-reduce(f32[2,1024]{1,0:T(2,128)S(1)} %bitcast.143), channel_id=1, replica_groups=mesh['dp'=16,'tensor'=4,'section'=4] {'dp','tensor'}, use_global_device_ids=true, to_apply=%region_4.0 | all-reduce | flops 2048 | bytes 16384 | tf_op jit(solution)/shard_map/psum | solution.py:92
  1078.2 1.3 add_divide_fusion.1
  1079.5 1.4 fusion.69
  1080.9 0.9 fusion.48
  1081.8 3.5 fusion.23
  1085.3 5.6 fusion.14
  1090.9 0.8 slice_bitcast_fusion
  (41 shorter events, 0.2 us)
Async XLA Ops:
  7.2 123.7 %reduce-scatter.4.cloned.1.call-start = ((), (), s32[]{:S(2)}) async-start(), calls=%async_computation.9 | async-start | bytes 2228224
  53.0 79.7 %copy-start.8 = (f32[1,1,64,1024]{3,2,1,0:T(8,128)S(1)}, f32[1,1,64,1024]{3,2,1,0:T(8,128)}, u32[]{:S(2)}) copy-start(f32[1,1,64,1024]{3,2,1,0:T(8,128)} %param.19) | copy-start | bytes 786436
  53.0 80.5 %copy-start.9 = (f32[1,1,64,1024]{3,2,1,0:T(8,128)S(1)}, f32[1,1,64,1024]{3,2,1,0:T(8,128)}, u32[]{:S(2)}) copy-start(f32[1,1,64,1024]{3,2,1,0:T(8,128)} %param.18) | copy-start | bytes 786436
  53.0 151.7 %copy-start.10 = (f32[1,1,64,1024]{3,2,1,0:T(8,128)S(1)}, f32[1,1,64,1024]{3,2,1,0:T(8,128)}, u32[]{:S(2)}) copy-start(f32[1,1,64,1024]{3,2,1,0:T(8,128)} %param.17) | copy-start | bytes 786436
  53.1 151.7 %all-gather.12.cloned.1.call-start = ((), (), s32[]{:S(2)}) async-start(), calls=%async_computation.3 | async-start | bytes 2228224 | tf_op jit(solution)/shard_map/all_gather | solution.py:58
  132.7 145.0 %all-gather.20.cloned.1.call-start = ((), (), s32[]{:S(2)}) async-start(), calls=%async_computation.7 | async-start | bytes 2228224 | tf_op jit(solution)/shard_map/all_gather | solution.py:56
  133.5 217.1 %all-gather.22.cloned.1.call-start = ((), (), s32[]{:S(2)}) async-start(), calls=%async_computation.8 | async-start | bytes 2228224 | tf_op jit(solution)/shard_map/all_gather | solution.py:55
  134.2 350.7 %all-gather.14.cloned.1.call-start = ((), (), s32[]{:S(2)}) async-start(), calls=%async_computation.4 | async-start | bytes 4456448 | tf_op jit(solution)/shard_map/all_gather | solution.py:86
  134.5 145.3 %copy-start.11 = (f32[1,1,64,1024]{3,2,1,0:T(8,128)S(1)}, f32[1,1,64,1024]{3,2,1,0:T(8,128)}, u32[]{:S(2)}) copy-start(f32[1,1,64,1024]{3,2,1,0:T(8,128)} %param.16) | copy-start | bytes 786436
  204.7 75.0 %copy-start.1 = (bf16[1,1024,1024]{2,1,0:T(8,128)(2,1)S(1)}, bf16[1,1024,1024]{2,1,0:T(8,128)(2,1)}, u32[]{:S(2)}) copy-start(bf16[1,1024,1024]{2,1,0:T(8,128)(2,1)} %all-gather.12.cloned.1.call-done) | copy-start | bytes 6291460
  207.2 73.4 %copy-start.6 = (f32[64,1024]{1,0:T(8,128)}, f32[64,1024]{1,0:T(8,128)S(1)}, u32[]{:S(2)}) copy-start(f32[64,1024]{1,0:T(8,128)S(1)} %fusion.20) | copy-start | bytes 786436
  280.6 105.9 %copy-start.7 = (f32[64,1024]{1,0:T(8,128)}, f32[64,1024]{1,0:T(8,128)S(1)}, u32[]{:S(2)}) copy-start(f32[64,1024]{1,0:T(8,128)S(1)} %fusion.17) | copy-start | bytes 786436
  280.6 105.9 %copy-start = (bf16[1,1,1024,1024]{3,2,1,0:T(8,128)(2,1)S(1)}, bf16[1,1,1024,1024]{3,2,1,0:T(8,128)(2,1)}, u32[]{:S(2)}) copy-start(bf16[1,1,1024,1024]{3,2,1,0:T(8,128)(2,1)} %all-gather.20.cloned.1.call-done) | copy-start | bytes 6291460
  280.6 105.9 %copy-start.3 = (bf16[1,1,64,1024]{3,2,1,0:T(8,128)(2,1)S(1)}, bf16[1,1,64,1024]{3,2,1,0:T(8,128)(2,1)}, u32[]{:S(2)}) copy-start(bf16[1,1,64,1024]{3,2,1,0:T(8,128)(2,1)} %convert_element_type.87) | copy-start | bytes 393220
  386.4 300.2 %all-reduce.3.cloned.1.call-start = ((), (), s32[]{:S(2)}) async-start(), calls=%async_computation.10 | async-start | bytes 8388608
  400.8 90.7 %copy-start.14 = (u32[256]{0:T(256)S(1)}, u32[256]{0:T(256)}, u32[]{:S(2)}) copy-start(u32[256]{0:T(256)} %constant.66) | copy-start | bytes 3076
  400.8 286.8 %copy-start.4 = (f32[1,1,64,1024]{3,2,1,0:T(8,128)S(1)}, f32[1,1,64,1024]{3,2,1,0:T(8,128)}, u32[]{:S(2)}) copy-start(f32[1,1,64,1024]{3,2,1,0:T(8,128)} %param.15) | copy-start | bytes 786436
  400.8 286.8 %copy-start.5 = (f32[1,1,64,1024]{3,2,1,0:T(8,128)S(1)}, f32[1,1,64,1024]{3,2,1,0:T(8,128)}, u32[]{:S(2)}) copy-start(f32[1,1,64,1024]{3,2,1,0:T(8,128)} %param.14) | copy-start | bytes 786436
  400.8 387.3 %all-gather.16.cloned.1.call-start = ((), (), s32[]{:S(2)}) async-start(), calls=%async_computation.5 | async-start | bytes 4456448 | tf_op jit(solution)/shard_map/all_gather | solution.py:86
  491.4 590.4 %all-gather.10.cloned.1.call-start = ((), (), s32[]{:S(2)}) async-start(), calls=%async_computation.2 | async-start | bytes 2228224 | tf_op jit(solution)/shard_map/all_gather | solution.py:73
  688.5 396.8 %all-gather.18.cloned.1.call-start = ((), (), s32[]{:S(2)}) async-start(), calls=%async_computation.6 | async-start | bytes 4456448 | tf_op jit(solution)/shard_map/all_gather | solution.py:86
  788.1 6.5 copy-start.13
  788.1 134.5 %copy-start.12 = (f32[1,1,1,2,1024]{4,3,2,1,0:T(2,128)S(1)}, f32[1,1,1,2,1024]{4,3,2,1,0:T(2,128)}, u32[]{:S(2)}) copy-start(f32[1,1,1,2,1024]{4,3,2,1,0:T(2,128)} %param.20) | copy-start | bytes 24580
  1081.8 3.5 copy-start.2
Sparse Core Ops, SparseCore 0:
  53.2 77.7 reduce-scatter.3
  133.3 71.4 all-gather.11
  207.1 70.5 all-gather.19
  279.9 70.5 all-gather.21
  386.5 98.3 all-gather.13
  487.4 199.1 all-reduce.2
  689.0 99.1 all-gather.15
  790.5 73.1 all-gather.9
  866.1 98.3 all-gather.17
where the time goes:
time: 1100 us
  waiting for transfers between devices  666 us (61%)
  blocking collectives  346 us (31%)
  matrix products  32.5 us (3%)
  local copies, waits for them, and re-layouts  31.6 us (3%)
  between operations  14.7 us (1%)
    unnamed x11, waiting for transfers between devices  272 us
    all_gather x3, waiting for transfers between devices, local(): iterate_full = lax.all_gather(iterate_half, 'dp', axis=1, tiled=True)  184 us
    psum x1, blocking collectives, local(): gain_sum = lax.psum(gain_grads[0, 0, 0], ('dp', 'tensor'))  156 us
    psum x1, blocking collectives, local(): table_sum = lax.psum(table_grads[0, 0], ('dp', 'section'))  128 us
    all_gather x1, waiting for transfers between devices, local(): lax.all_gather(right_local, 'dp', axis=1, tiled=True)  70.5 us
    all_gather x1, waiting for transfers between devices, local(): grad_full = lax.all_gather(grad_rows, 'dp', axis=1, tiled=True)  70.3 us
    all_gather x1, waiting for transfers between devices, local(): lax.all_gather(left_local, 'dp', axis=1, tiled=True)  69.9 us
    psum x1, blocking collectives, local(): squares = lax.psum(jnp.sum(power * power, axis=(1, 2)), 'dp')  32.8 us
  transfers between devices with their start and end apart: 9, of which 7 were waited for; matrix products, arithmetic and copies ran while one was open for 4% of the time, Pallas kernels for 0%

commit v1 on v0

--- a/solution.py
+++ b/solution.py
@@ -93,7 +93,8 @@
     gain_moment = beta_first * gain_first[0] + (1.0 - beta_first) * gain_sum
     gain_squares = beta_second * gain_second[0] + (1.0 - beta_second) * gain_sum * gain_sum
     gain_update = adam_direction(gain_moment, gain_squares)
-    table_sum = lax.psum(table_grads[0, 0], ("dp", "section"))
+    _attach_cube = lambda obj: jnp.sum(jax.lax.all_gather(obj, ("dp", "section")), 0)
+    table_sum = _attach_cube(table_grads[0, 0])
     table_moment = beta_first * table_first + (1.0 - beta_first) * table_sum
     table_squares = beta_second * table_second + (1.0 - beta_second) * table_sum * table_sum
     table_update = adam_direction(table_moment, table_squares)

time: 1100 us -> 1050 us (0.955)
  blocking collectives: 346 us -> 297 us
    psum x1 -> x0, blocking collectives: 128 us -> none  [local(): table_sum = lax.psum(table_grads[0, 0], ('dp', 'section'))]
    all_gather x0 -> x1, blocking collectives: none -> 77.8 us  [local(): jax.lax.all_gather(obj, ('dp', 'section'))]
where the time goes in v1:
time: 1050 us
  waiting for transfers between devices  666 us (63%)
  blocking collectives  297 us (28%)
  matrix products  32.5 us (3%)
  local copies, waits for them, and re-layouts  31.6 us (3%)
  between operations  14.7 us (1%)
    unnamed x11, waiting for transfers between devices  272 us
    all_gather x3, waiting for transfers between devices, local(): iterate_full = lax.all_gather(iterate_half, 'dp', axis=1, tiled=True)  184 us
    psum x1, blocking collectives, local(): gain_sum = lax.psum(gain_grads[0, 0, 0], ('dp', 'tensor'))  157 us
    all_gather x1, blocking collectives, local(): jax.lax.all_gather(obj, ('dp', 'section'))  77.8 us
    all_gather x1, waiting for transfers between devices, local(): lax.all_gather(right_local, 'dp', axis=1, tiled=True)  70.5 us
    all_gather x1, waiting for transfers between devices, local(): grad_full = lax.all_gather(grad_rows, 'dp', axis=1, tiled=True)  70.3 us
    all_gather x1, waiting for transfers between devices, local(): lax.all_gather(left_local, 'dp', axis=1, tiled=True)  69.9 us
    psum x1, blocking collectives, local(): squares = lax.psum(jnp.sum(power * power, axis=(1, 2)), 'dp')  32.8 us
  transfers between devices with their start and end apart: 9, of which 7 were waited for; matrix products, arithmetic and copies ran while one was open for 4% of the time, Pallas kernels for 0%

profile of v1, /device:TPU:2, one launch (start us, length us, event | category | flops | bytes accessed | tf_op | source)
XLA Modules:
  0.0 1050.2 jit_solution(16243675834636730887)
XLA Ops:
  7.2 0.0 reduce-scatter.4.cloned.1.call-start
  7.2 4.0 copy.47
  11.2 29.7 %all_to_all.18 = bf16[4,1024,256]{1,2,0:T(8,128)(2,1)S(1)} all-to-all(bf16[4,1024,256]{1,2,0:T(8,128)(2,1)} %bitcast.139), channel_id=1, replica_groups=mesh['dp'=16,'tensor'=4,'section'=4] {'tensor'}, dimensions={0} | all-to-all | bytes 4194304 | tf_op jit(solution)/shard_map/all_to_all | solution.py:45
  40.9 7.8 copy.50
  48.7 4.4 copy.60
  53.1 0.0 all-gather.13.cloned.1.call-start
  53.1 77.8 %reduce-scatter.4.cloned.1.call-done = bf16[64,1024]{1,0:T(8,128)(2,1)} async-done(((bf16[1024,1024]{1,0:T(8,128)(2,1)}), bf16[64,1024]{1,0:T(8,128)(2,1)}) %reduce-scatter.4.cloned.1.call-update) | async-done | bytes 131088
  130.9 1.0 reshape_bitcast_fusion
  132.0 0.7 copy.49
  132.7 0.0 all-gather.21.cloned.1.call-start
  132.8 0.7 convert_element_type.84
  133.5 0.0 all-gather.23.cloned.1.call-start
  133.5 0.7 convert_element_type.87
  134.2 0.0 all-gather.15.cloned.1.call-start
  134.3 0.2 copy.51
  134.5 70.3 %all-gather.13.cloned.1.call-done = bf16[1,1024,1024]{2,1,0:T(8,128)(2,1)} async-done(((bf16[1,64,1024]{2,1,0:T(8,128)(2,1)}), bf16[1,1024,1024]{2,1,0:T(8,128)(2,1)}) %all-gather.13.cloned.1.call-update) | async-done | bytes 2097168 | tf_op jit(solution)/shard_map/all_gather | solution.py:58
  204.7 2.4 fusion.20
  207.2 70.5 %all-gather.21.cloned.1.call-done = bf16[1,1,1024,1024]{3,2,1,0:T(8,128)(2,1)} async-done(((bf16[1,1,64,1024]{3,2,1,0:T(8,128)(2,1)}), bf16[1,1,1024,1024]{3,2,1,0:T(8,128)(2,1)}) %all-gather.21.cloned.1.call-update) | async-done | bytes 2097168 | tf_op jit(solution)/shard_map/all_gather | solution.py:56
  277.7 2.1 fusion.26
  279.8 0.8 fusion.17
  280.6 69.9 %all-gather.23.cloned.1.call-done = bf16[1,1,1024,1024]{3,2,1,0:T(8,128)(2,1)} async-done(((bf16[1,1,64,1024]{3,2,1,0:T(8,128)(2,1)}), bf16[1,1,1024,1024]{3,2,1,0:T(8,128)(2,1)}) %all-gather.23.cloned.1.call-update) | async-done | bytes 2097168 | tf_op jit(solution)/shard_map/all_gather | solution.py:55
  350.5 2.1 fusion.29
  352.6 0.2 multiply_reduce_fusion
  352.8 32.8 %psum.14 = f32[2]{0:T(128)S(1)} all-reduce(f32[2]{0:T(128)S(1)} %multiply_reduce_fusion), channel_id=1, replica_groups=mesh['dp'=16,'tensor'=4,'section'=4] {'dp'}, use_global_device_ids=true, to_apply=%region_3.0 | all-reduce | flops 2 | bytes 16 | tf_op jit(solution)/shard_map/psum | solution.py:82
  385.6 0.8 fusion.68
  386.4 0.0 all-reduce.3.cloned.1.call-start
  386.5 3.2 convolution_bitcast_fusion
  389.7 11.0 %copy.48 = f32[1024,1,1024]{2,1,0:T(1,128)} copy(f32[1024,1,1024]{0,2,1:T(8,128)} %convolution_bitcast_fusion) | data formatting | bytes 8388608 | tf_op jit(solution)/shard_map/mkc,mkj->cmj/transpose | solution.py:20
  400.8 0.0 all-gather.17.cloned.1.call-start
  400.9 84.0 %all-gather.15.cloned.1.call-done = bf16[2,1024,1024]{2,1,0:T(8,128)(2,1)} async-done(((bf16[2,64,1024]{2,1,0:T(8,128)(2,1)}), bf16[2,1024,1024]{2,1,0:T(8,128)(2,1)}) %all-gather.15.cloned.1.call-update) | async-done | bytes 4194320 | tf_op jit(solution)/shard_map/all_gather | solution.py:86
  484.9 6.5 fusion.73
  491.4 0.0 all-gather.11.cloned.1.call-start
  491.5 0.6 dynamic-slice
  492.7 193.9 %all-reduce.3.cloned.1.call-done = f32[1024,1,1024]{2,1,0:T(1,128)} async-done(((f32[1024,1,1024]{2,1,0:T(1,128)}), f32[1024,1,1024]{2,1,0:T(1,128)}) %all-reduce.3.cloned.1.call-update) | async-done | bytes 4194320
  686.6 1.0 constant_dynamic-slice_fusion
  687.6 0.8 fusion.57
  688.4 0.0 all-gather.19.cloned.1.call-start
  688.5 99.6 %all-gather.17.cloned.1.call-done = bf16[2,1024,1024]{2,1,0:T(8,128)(2,1)} async-done(((bf16[2,64,1024]{2,1,0:T(8,128)(2,1)}), bf16[2,1024,1024]{2,1,0:T(8,128)(2,1)}) %all-gather.17.cloned.1.call-update) | async-done | bytes 4194320 | tf_op jit(solution)/shard_map/all_gather | solution.py:86
  788.1 6.5 fusion.76
  794.6 77.8 %all-gather.2 = f32[64,1,32,4]{2,3,1,0:T(4,128)} all-gather(f32[1,1,32,4]{2,3,1,0:T(4,128)S(1)} %copy-done.12), channel_id=4, replica_groups=mesh['dp'=16,'tensor'=4,'section'=4] {'dp','section'}, dimensions={0}, use_global_device_ids=true | all-gather | bytes 33280 | tf_op jit(solution)/shard_map/all_gather | solution.py:96
  872.4 1.0 reduce_sum.19
  873.3 156.9 %psum.15 = f32[2,1024]{1,0:T(2,128)S(1)} all-reduce(f32[2,1024]{1,0:T(2,128)} %bitcast.142), channel_id=1, replica_groups=mesh['dp'=16,'tensor'=4,'section'=4] {'dp','tensor'}, use_global_device_ids=true, to_apply=%region_4.0 | all-reduce | flops 2048 | bytes 16384 | tf_op jit(solution)/shard_map/psum | solution.py:92
  1030.2 1.3 add_divide_fusion.1
  1031.5 1.4 fusion.69
  1032.9 0.9 fusion.48
  1033.8 3.5 fusion.23
  1037.3 5.6 fusion.14
  1042.9 0.8 slice_bitcast_fusion
  (42 shorter events, 0.2 us)
Async XLA Ops:
  7.2 123.7 %reduce-scatter.4.cloned.1.call-start = ((), (), s32[]{:S(2)}) async-start(), calls=%async_computation.9 | async-start | bytes 2228224
  53.0 79.7 %copy-start.8 = (f32[1,1,64,1024]{3,2,1,0:T(8,128)S(1)}, f32[1,1,64,1024]{3,2,1,0:T(8,128)}, u32[]{:S(2)}) copy-start(f32[1,1,64,1024]{3,2,1,0:T(8,128)} %param.19) | copy-start | bytes 786436
  53.0 80.5 %copy-start.9 = (f32[1,1,64,1024]{3,2,1,0:T(8,128)S(1)}, f32[1,1,64,1024]{3,2,1,0:T(8,128)}, u32[]{:S(2)}) copy-start(f32[1,1,64,1024]{3,2,1,0:T(8,128)} %param.18) | copy-start | bytes 786436
  53.0 151.7 %copy-start.10 = (f32[1,1,64,1024]{3,2,1,0:T(8,128)S(1)}, f32[1,1,64,1024]{3,2,1,0:T(8,128)}, u32[]{:S(2)}) copy-start(f32[1,1,64,1024]{3,2,1,0:T(8,128)} %param.17) | copy-start | bytes 786436
  53.1 151.7 %all-gather.13.cloned.1.call-start = ((), (), s32[]{:S(2)}) async-start(), calls=%async_computation.3 | async-start | bytes 2228224 | tf_op jit(solution)/shard_map/all_gather | solution.py:58
  132.7 145.0 %all-gather.21.cloned.1.call-start = ((), (), s32[]{:S(2)}) async-start(), calls=%async_computation.7 | async-start | bytes 2228224 | tf_op jit(solution)/shard_map/all_gather | solution.py:56
  133.5 217.1 %all-gather.23.cloned.1.call-start = ((), (), s32[]{:S(2)}) async-start(), calls=%async_computation.8 | async-start | bytes 2228224 | tf_op jit(solution)/shard_map/all_gather | solution.py:55
  134.2 350.7 %all-gather.15.cloned.1.call-start = ((), (), s32[]{:S(2)}) async-start(), calls=%async_computation.4 | async-start | bytes 4456448 | tf_op jit(solution)/shard_map/all_gather | solution.py:86
  134.5 145.3 %copy-start.11 = (f32[1,1,64,1024]{3,2,1,0:T(8,128)S(1)}, f32[1,1,64,1024]{3,2,1,0:T(8,128)}, u32[]{:S(2)}) copy-start(f32[1,1,64,1024]{3,2,1,0:T(8,128)} %param.16) | copy-start | bytes 786436
  204.7 75.0 %copy-start.1 = (bf16[1,1024,1024]{2,1,0:T(8,128)(2,1)S(1)}, bf16[1,1024,1024]{2,1,0:T(8,128)(2,1)}, u32[]{:S(2)}) copy-start(bf16[1,1024,1024]{2,1,0:T(8,128)(2,1)} %all-gather.13.cloned.1.call-done) | copy-start | bytes 6291460
  207.2 73.4 %copy-start.6 = (f32[64,1024]{1,0:T(8,128)}, f32[64,1024]{1,0:T(8,128)S(1)}, u32[]{:S(2)}) copy-start(f32[64,1024]{1,0:T(8,128)S(1)} %fusion.20) | copy-start | bytes 786436
  280.6 105.9 %copy-start.7 = (f32[64,1024]{1,0:T(8,128)}, f32[64,1024]{1,0:T(8,128)S(1)}, u32[]{:S(2)}) copy-start(f32[64,1024]{1,0:T(8,128)S(1)} %fusion.17) | copy-start | bytes 786436
  280.6 105.9 %copy-start = (bf16[1,1,1024,1024]{3,2,1,0:T(8,128)(2,1)S(1)}, bf16[1,1,1024,1024]{3,2,1,0:T(8,128)(2,1)}, u32[]{:S(2)}) copy-start(bf16[1,1,1024,1024]{3,2,1,0:T(8,128)(2,1)} %all-gather.21.cloned.1.call-done) | copy-start | bytes 6291460
  280.6 105.9 %copy-start.3 = (bf16[1,1,64,1024]{3,2,1,0:T(8,128)(2,1)S(1)}, bf16[1,1,64,1024]{3,2,1,0:T(8,128)(2,1)}, u32[]{:S(2)}) copy-start(bf16[1,1,64,1024]{3,2,1,0:T(8,128)(2,1)} %convert_element_type.87) | copy-start | bytes 393220
  386.4 300.2 %all-reduce.3.cloned.1.call-start = ((), (), s32[]{:S(2)}) async-start(), calls=%async_computation.10 | async-start | bytes 8388608
  400.8 90.7 %copy-start.14 = (u32[256]{0:T(256)S(1)}, u32[256]{0:T(256)}, u32[]{:S(2)}) copy-start(u32[256]{0:T(256)} %constant.66) | copy-start | bytes 3076
  400.8 286.8 %copy-start.4 = (f32[1,1,64,1024]{3,2,1,0:T(8,128)S(1)}, f32[1,1,64,1024]{3,2,1,0:T(8,128)}, u32[]{:S(2)}) copy-start(f32[1,1,64,1024]{3,2,1,0:T(8,128)} %param.15) | copy-start | bytes 786436
  400.8 286.8 %copy-start.5 = (f32[1,1,64,1024]{3,2,1,0:T(8,128)S(1)}, f32[1,1,64,1024]{3,2,1,0:T(8,128)}, u32[]{:S(2)}) copy-start(f32[1,1,64,1024]{3,2,1,0:T(8,128)} %param.14) | copy-start | bytes 786436
  400.8 387.3 %all-gather.17.cloned.1.call-start = ((), (), s32[]{:S(2)}) async-start(), calls=%async_computation.5 | async-start | bytes 4456448 | tf_op jit(solution)/shard_map/all_gather | solution.py:86
  491.4 542.4 %all-gather.11.cloned.1.call-start = ((), (), s32[]{:S(2)}) async-start(), calls=%async_computation.2 | async-start | bytes 2228224 | tf_op jit(solution)/shard_map/all_gather | solution.py:73
  688.4 348.8 %all-gather.19.cloned.1.call-start = ((), (), s32[]{:S(2)}) async-start(), calls=%async_computation.6 | async-start | bytes 4456448 | tf_op jit(solution)/shard_map/all_gather | solution.py:86
  788.1 6.5 copy-start.12
  788.1 242.1 %copy-start.13 = (f32[32,4]{0,1:T(4,128)S(1)}, f32[32,4]{0,1:T(4,128)}, u32[]{:S(2)}) copy-start(f32[32,4]{0,1:T(4,128)} %param.24) | copy-start | bytes 1540
  1033.8 3.5 copy-start.2
Sparse Core Ops, SparseCore 0:
  53.2 77.7 reduce-scatter.3
  133.3 71.4 all-gather.12
  207.1 70.5 all-gather.20
  279.9 70.5 all-gather.22
  386.5 98.2 all-gather.14
  487.4 199.1 all-reduce.2
  689.0 99.1 all-gather.16
  790.5 72.3 all-gather.10
  865.2 97.3 all-gather.18
